TPU v7x, 256 devices: a whole 4x4x8 slice. The times are simulated.
256 devices in a mesh: pipe: 2 (over core), expert: 16 (over y, x), dp: 8 (over z).
Axes of the slice: x: 4, y: 4, z: 8, core: 2. Of those that a mesh axis runs over, the one named last changes fastest.
Arguments:
- tokens: bfloat16 [2048, 6144], P('expert'), may hold values from -6 to 6
- expert_ids: int32 [2048, 2], P('expert'), may hold values from 0 to 15, all different within a row; in each aligned block of 128 rows (0 to 127, 128 to 255, ...) at most 24 rows name the same one
- w_router: bfloat16 [6144, 16], replicated, may hold values from -0.078125 to 0.078125
- w_gate: bfloat16 [16, 6144, 4096], P('expert', None, ('pipe', 'dp')), may hold values from -0.078125 to 0.078125
- w_up: bfloat16 [16, 6144, 4096], P('expert', None, ('pipe', 'dp')), may hold values from -0.078125 to 0.078125
- w_down: bfloat16 [16, 4096, 6144], P('expert', ('pipe', 'dp')), may hold values from -0.125 to 0.125
Outputs:
- mixed: bfloat16 [2048, 6144], P('expert', ('pipe', 'dp'))
Inputs may be any that keep to these rules, and one draw needn't show every extreme that they name: `expert_ids`: in each aligned block of 128 tokens no expert is named by more than 24 of the block's choices, a bound that some block reaches; the two experts of a token differ.
All inputs are finite; a program needn't handle non-finite values.
Results may differ from a plain program's by a relative error of at most 0.018.
Values may be sent and summed in bfloat16 or wider, within the bound.
A program may use at most 64 MiB of HBM per device.

v0:
```python
import jax
import jax.numpy as jnp
from jax import lax
from jax.sharding import PartitionSpec as P


def slots_of(ids, experts):
    blocks = ids.shape[0]
    flat = ids.reshape(blocks, -1)
    onehot = (flat[:, :, None] == jnp.arange(experts, dtype=jnp.int32)[None, None, :]).astype(
        jnp.int32
    )
    before = jnp.cumsum(onehot, axis=1) - onehot
    slot = jnp.sum(before * onehot, axis=-1)
    return (flat, slot)


def dispatch(x_rows, id_rows, experts, capacity):
    count, width = x_rows.shape
    topk = id_rows.shape[1]
    flat, slot = slots_of(id_rows[None], experts)
    dest = flat[0] * capacity + slot[0]
    select = (jnp.arange(experts * capacity, dtype=jnp.int32)[:, None] == dest[None, :]).astype(
        jnp.bfloat16
    )
    repeated = jnp.repeat(x_rows, topk, axis=0)
    placed = jnp.dot(select, repeated, preferred_element_type=jnp.float32).astype(jnp.bfloat16)
    return (placed.reshape(experts, capacity, width), dest)


def body(tokens, expert_ids, w_router, w_gate, w_up, w_down):
    count, width = tokens.shape
    topk = expert_ids.shape[1]
    experts = lax.axis_size("expert") * w_gate.shape[0]
    capacity = 3 * count * topk // (2 * experts)
    groups = lax.axis_size(("pipe", "dp"))
    columns = width // groups
    start = lax.axis_index(("pipe", "dp")) * columns
    mine = lax.dynamic_slice_in_dim(tokens, start, columns, 1)
    local, dest = dispatch(mine, expert_ids, experts, capacity)
    arrived = lax.all_to_all(local, "expert", split_axis=0, concat_axis=0, tiled=True)
    arrived = arrived.reshape(experts * capacity, columns)
    inputs = lax.all_gather(arrived, ("pipe", "dp"), axis=1, tiled=True)
    gate = jnp.dot(inputs, w_gate[0], preferred_element_type=jnp.float32)
    upper = jnp.dot(inputs, w_up[0], preferred_element_type=jnp.float32)
    hidden = (jax.nn.silu(gate) * upper).astype(jnp.bfloat16)
    term = jnp.dot(hidden, w_down[0], preferred_element_type=jnp.float32).astype(jnp.bfloat16)
    logits = jnp.dot(tokens, w_router, preferred_element_type=jnp.float32)
    chosen = jnp.take_along_axis(logits, expert_ids, axis=1)
    first = jax.nn.sigmoid(chosen[:, 0] - chosen[:, 1])
    gates = jnp.stack([first, 1.0 - first], axis=1)
    summed = lax.psum_scatter(term, ("pipe", "dp"), scatter_dimension=1, tiled=True)
    returned = lax.all_to_all(
        summed.reshape(experts, capacity, columns),
        "expert",
        split_axis=0,
        concat_axis=0,
        tiled=True,
    )
    picked = jnp.take(returned.reshape(experts * capacity, columns), dest, axis=0)
    picked = picked.reshape(count, topk, columns).astype(jnp.float32)
    return jnp.sum(gates[:, :, None] * picked, axis=1).astype(jnp.bfloat16)


def solution(mesh):
    placed = (
        P("expert", None),
        P("expert", None),
        P(),
        P("expert", None, ("pipe", "dp")),
        P("expert", None, ("pipe", "dp")),
        P("expert", ("pipe", "dp"), None),
    )
    return jax.shard_map(
        body, mesh=mesh, in_specs=placed, out_specs=P("expert", ("pipe", "dp")), check_vma=False
    )
```

profile of v0, /device:TPU:1, one launch (start us, length us, event | category | flops | bytes accessed | tf_op | source)
XLA Modules:
  0.0 195.6 jit_solution(6473342927977986380)
XLA Ops:
  6.5 0.9 copy.45
  7.5 0.1 eq.40
  7.7 0.6 reduce-window.6
  8.2 0.8 slice_reduce_fusion
  9.0 0.9 constant_dynamic-slice_fusion
  10.1 0.7 reduce-window.9
  11.0 0.7 fusion.20
  11.8 0.6 copy-done.3
  12.3 0.7 multiply_add_fusion
  13.0 0.3 convolution_convert_fusion.1
  13.3 15.7 %all_to_all.10 = bf16[16,24,384]{2,1,0:T(8,128)(2,1)} all-to-all(bf16[16,24,384]{2,1,0:T(8,128)(2,1)S(1)} %bitcast.50), channel_id=1, replica_groups=mesh['pipe'=2,'expert'=16,'dp'=8] {'expert'}, dimensions={0} | all-to-all | bytes 589824 | tf_op jit(solution)/shard_map/all_to_all | solution.py:41
  29.0 43.7 %all-gather.2.cloned.1.call-done = bf16[384,6144]{1,0:T(8,128)(2,1)} async-done(((bf16[384,384]{1,0:T(8,128)(2,1)}), bf16[384,6144]{1,0:T(8,128)(2,1)}) %all-gather.2.cloned.1.call-update) | async-done | bytes 4718608 | tf_op jit(solution)/shard_map/all_gather | solution.py:43
  72.8 4.7 %fusion.3 = f32[384,256]{1,0:T(8,128)S(1)} fusion(bf16[384,6144]{1,0:T(8,128)(2,1)} %all-gather.2.cloned.1.call-done, bf16[1,6144,256]{2,1,0:T(8,128)(2,1)} %param.9), kind=kOutput, calls=%fused_computation.6 | convolution fusion | flops 1207959552 | bytes 8257536 | tf_op jit(solution)/shard_map/dot_general | solution.py:44
  77.5 10.6 %convolution_convert_fusion = bf16[384,6144]{1,0:T(8,128)(2,1)} fusion(bf16[1,256,6144]{2,1,0:T(8,128)(2,1)S(1)} %copy-done, bf16[384,6144]{1,0:T(8,128)(2,1)} %all-gather.2.cloned.1.call-done, bf16[1,6144,256]{2,1,0:T(8,128)(2,1)} %param.10, f32[384,256]{1,0:T(8,128)S(1)} %fusion.3), kind=kOutput, calls=%fused_computation.2 | convolution fusion | flops 2418868224 | bytes 16121856 | tf_op jit(solution)/shard_map/dot_general | solution.py:47
  88.0 6.6 %copy.52 = bf16[384,6144]{0,1:T(8,128)(2,1)} copy(bf16[384,6144]{1,0:T(8,128)(2,1)} %convolution_convert_fusion) | data formatting | bytes 9437184
  94.7 0.6 copy-done.4
  95.3 0.1 reduce_sum.23
  95.5 0.1 copy.51
  95.6 0.1 mul.61
  95.8 0.1 copy.50
  96.0 0.1 copy.42
  96.1 0.1 reshape.211
  96.3 1.9 fusion.22
  98.2 2.0 %gather_fusion.1 = f32[256]{0:T(256)S(1)} fusion(f32[128,16]{0,1:T(8,128)S(1)} %fusion.22, s32[256]{0:T(256)S(1)} %reshape.211), kind=kCustom, calls=%fused_computation.1 | custom fusion | bytes 4096 | tf_op jit(solution)/shard_map/jit(take_along_axis)/gather | solution.py:49
  100.2 0.1 reshape.214
  100.5 67.4 %reduce-scatter.4.cloned.1.call-done = bf16[384,384]{1,0:T(8,128)(2,1)} async-done(((bf16[6144,384]{1,0:T(8,128)(2,1)}), bf16[384,384]{1,0:T(8,128)(2,1)}) %reduce-scatter.4.cloned.1.call-update) | async-done | bytes 294928
  168.0 1.8 copy.53
  169.8 6.3 %all-to-all-start.1 = ((bf16[16,24,384]{2,1,0:T(8,128)(2,1)}), bf16[16,24,384]{2,1,0:T(8,128)(2,1)S(1)}, u32[]{:S(2)}, u32[]{:S(2)}) async-start(bf16[16,24,384]{2,1,0:T(8,128)(2,1)} %bitcast.49), calls=%async_computation.1 | async-start | bytes 589824 | tf_op jit(solution)/shard_map/all_to_all | solution.py:53
  176.2 8.5 %all-to-all-done.1 = bf16[16,24,384]{2,1,0:T(8,128)(2,1)S(1)} async-done(((bf16[16,24,384]{2,1,0:T(8,128)(2,1)}), bf16[16,24,384]{2,1,0:T(8,128)(2,1)S(1)}, u32[]{:S(2)}, u32[]{:S(2)}) %all-to-all-start.1) | async-done | bytes 294944 | tf_op jit(solution)/shard_map/all_to_all | solution.py:53
  184.6 1.8 gather_fusion
  186.5 1.0 gather.12
  187.5 1.3 multiply_reduce_fusion
  (33 shorter events, 0.8 us)
Async XLA Ops:
  6.5 70.9 %copy-start = (bf16[1,256,6144]{2,1,0:T(8,128)(2,1)S(1)}, bf16[1,256,6144]{2,1,0:T(8,128)(2,1)}, u32[]{:S(2)}) copy-start(bf16[1,256,6144]{2,1,0:T(8,128)(2,1)} %param.11) | copy-start | bytes 9437188
  6.5 66.2 %all-gather.2.cloned.1.call-start = ((), (), s32[]{:S(2)}) async-start(), calls=%async_computation.3 | async-start | bytes 5013504 | tf_op jit(solution)/shard_map/all_gather | solution.py:43
  7.6 1.4 copy-start.5
  11.8 0.6 copy-start.3
  29.0 139.0 %reduce-scatter.4.cloned.1.call-start = ((), (), s32[]{:S(2)}) async-start(), calls=%async_computation.4 | async-start | bytes 5013504
  94.7 0.7 copy-start.4
  94.7 0.8 copy-start.2
  94.7 1.6 copy-start.1
  169.8 14.8 %all-to-all-start.1 = ((bf16[16,24,384]{2,1,0:T(8,128)(2,1)}), bf16[16,24,384]{2,1,0:T(8,128)(2,1)S(1)}, u32[]{:S(2)}, u32[]{:S(2)}) async-start(bf16[16,24,384]{2,1,0:T(8,128)(2,1)} %bitcast.49), calls=%async_computation.1 | async-start | bytes 589824 | tf_op jit(solution)/shard_map/all_to_all | solution.py:53
Sparse Core Ops, SparseCore 0:
  29.1 43.6 all-gather.1
  94.8 73.1 reduce-scatter.3
where the time goes:
time: 196 us
  waiting for transfers between devices  120 us (61%)
  local copies, waits for them, and re-layouts  18.7 us (10%)
  matrix products  17.4 us (9%)
  blocking collectives  15.7 us (8%)
  between operations  13.6 us (7%)
  starting transfers between devices  6.36 us (3%)
  other arithmetic  4.13 us (2%)
    unnamed x3, waiting for transfers between devices  67.5 us
    all_gather x1, waiting for transfers between devices, body(): inputs = lax.all_gather(arrived, ('pipe', 'dp'), axis=1, tiled=True)  43.7 us
    all_to_all x1, blocking collectives, body(): lax.all_to_all(local, 'expert', split_axis=0, concat_axis=0, tiled=True)  15.7 us
    unnamed x15, local copies, waits for them, and re-layouts  10.6 us
    dot_general x1, matrix products, body(): jnp.dot(hidden, w_down[0], preferred_element_type=jnp.float32)  10.6 us
    all_to_all x1, waiting for transfers between devices, body(): lax.all_to_all(summed.reshape(experts, capacity, columns), 'expert', spli...  8.47 us
    all_to_all x1, starting transfers between devices, body(): lax.all_to_all(summed.reshape(experts, capacity, columns), 'expert', spli...  6.32 us
    dot_general x1, matrix products, body(): gate = jnp.dot(inputs, w_gate[0], preferred_element_type=jnp.float32)  4.71 us
  transfers between devices with their start and end apart: 3, of which 3 were waited for; matrix products, arithmetic and copies ran while one was open for 3% of the time, Pallas kernels for 0%

commit v1 on v0

--- a/solution.py
+++ b/solution.py
@@ -40,7 +40,24 @@
     local, dest = dispatch(mine, expert_ids, experts, capacity)
     arrived = lax.all_to_all(local, "expert", split_axis=0, concat_axis=0, tiled=True)
     arrived = arrived.reshape(experts * capacity, columns)
-    inputs = lax.all_gather(arrived, ("pipe", "dp"), axis=1, tiled=True)
+    mat_out = lax.axis_size(("pipe", "dp"))
+    z, item_now, later = (mat_out, lax.axis_index(("pipe", "dp")), arrived.shape[1])
+    tray = [(w, (w + 1) % z) for w in range(z)]
+    ledger = [(w, (w - 1) % z) for w in range(z)]
+    inputs = jnp.zeros((*arrived.shape[:1], z * later, *arrived.shape[1 + 1 :]), arrived.dtype)
+    inputs = lax.dynamic_update_slice_in_dim(inputs, arrived, item_now * later, axis=1)
+    v_next = w_next = arrived
+    ready = z // 2
+    k = 1
+    while k < ready + 1:
+        v_next = lax.ppermute(v_next, axis_name=("pipe", "dp"), perm=tray)
+        inputs = lax.dynamic_update_slice_in_dim(inputs, v_next, (item_now - k) % z * later, axis=1)
+        if k < z - ready:
+            w_next = lax.ppermute(w_next, ("pipe", "dp"), ledger)
+            inputs = lax.dynamic_update_slice_in_dim(
+                inputs, w_next, (item_now + k) % z * later, axis=1
+            )
+        k += 1
     gate = jnp.dot(inputs, w_gate[0], preferred_element_type=jnp.float32)
     upper = jnp.dot(inputs, w_up[0], preferred_element_type=jnp.float32)
     hidden = (jax.nn.silu(gate) * upper).astype(jnp.bfloat16)

time: 196 us -> 227 us (1.16)
  starting transfers between devices: 6.36 us -> 36.3 us
  local copies, waits for them, and re-layouts: 18.7 us -> 27.1 us
  waiting for transfers between devices: 120 us -> 116 us
  matrix products: 17.4 us -> 14.1 us
    all_gather x1 -> x0, waiting for transfers between devices: 43.7 us -> none  [body(): inputs = lax.all_gather(arrived, ('pipe', 'dp'), axis=1, tiled=True)]
    ppermute x0 -> x15, waiting for transfers between devices: none -> 42.7 us  [the longest x7 24.7 us: body(): w_next = lax.ppermute(w_next, ('pipe', 'dp'), ledger)]
    ppermute x0 -> x15, starting transfers between devices: none -> 29.7 us  [the longest x7 27.8 us: body(): w_next = lax.ppermute(w_next, ('pipe', 'dp'), ledger)]
    dynamic_update_slice x0 -> x16, local copies, waits for them, and re-layouts: none -> 4.87 us  [the longest x8 2.43 us: body(): lax.dynamic_update_slice_in_dim(inputs, v_next, (item_now - k) % z * late...]
    dot_general x1, matrix products: 4.71 us -> 1.42 us  [body(): upper = jnp.dot(inputs, w_up[0], preferred_element_type=jnp.float32)]
    unnamed x15 -> x27, local copies, waits for them, and re-layouts: 10.6 us -> 13.6 us
    unnamed x3 -> x2, waiting for transfers between devices: 67.5 us -> 64.6 us
  transfers between devices with their start and end apart: 3 -> 17, of which waited for: 3 -> 15; matrix products, arithmetic and copies ran while one was open for 3% -> 5% of each run, Pallas kernels for 0% -> 0%
where the time goes in v1:
time: 227 us
  waiting for transfers between devices  116 us (51%)
  starting transfers between devices  36.3 us (16%)
  local copies, waits for them, and re-layouts  27.1 us (12%)
  blocking collectives  15.5 us (7%)
  matrix products  14.1 us (6%)
  between operations  13.8 us (6%)
  other arithmetic  4.1 us (2%)
    unnamed x2, waiting for transfers between devices  64.6 us
    ppermute x7, starting transfers between devices, body(): w_next = lax.ppermute(w_next, ('pipe', 'dp'), ledger)  27.8 us
    ppermute x7, waiting for transfers between devices, body(): w_next = lax.ppermute(w_next, ('pipe', 'dp'), ledger)  24.7 us
    ppermute x8, waiting for transfers between devices, body(): v_next = lax.ppermute(v_next, axis_name=('pipe', 'dp'), perm=tray)  18.1 us
    all_to_all x1, blocking collectives, body(): lax.all_to_all(local, 'expert', split_axis=0, concat_axis=0, tiled=True)  15.5 us
    unnamed x27, local copies, waits for them, and re-layouts  13.6 us
    dot_general x1, matrix products, body(): jnp.dot(hidden, w_down[0], preferred_element_type=jnp.float32)  10.5 us
    all_to_all x1, waiting for transfers between devices, body(): lax.all_to_all(summed.reshape(experts, capacity, columns), 'expert', spli...  8.39 us
  transfers between devices with their start and end apart: 17, of which 15 were waited for; matrix products, arithmetic and copies ran while one was open for 5% of the time, Pallas kernels for 0%

profile of v1, /device:TPU:1, one launch (start us, length us, event | category | flops | bytes accessed | tf_op | source)
XLA Modules:
  0.0 226.8 jit_solution(17767299399627187138)
XLA Ops:
  13.3 15.5 %all_to_all.10 = bf16[16,24,384]{2,1,0:T(8,128)(2,1)S(1)} all-to-all(bf16[16,24,384]{2,1,0:T(8,128)(2,1)S(1)} %bitcast.50), channel_id=1, replica_groups=mesh['pipe'=2,'expert'=16,'dp'=8] {'expert'}, dimensions={0} | all-to-all | bytes 589824 | tf_op jit(solution)/shard_map/all_to_all | solution.py:41
  28.8 1.6 collective-permute-start
  30.4 5.6 %collective-permute-start.1 = (bf16[384,384]{1,0:T(8,128)(2,1)S(1)}, bf16[384,384]{1,0:T(8,128)(2,1)S(1)}, u32[]{:S(2)}, u32[]{:S(2)}) collective-permute-start(bf16[384,384]{1,0:T(8,128)(2,1)S(1)} %bitcast.48), channel_id=1, source_target_pairs={{0,135},{1,0},{2,1},{3,2},{4,3},{5,4},{6,5},{7,6},{128,7},{129,128... | collective-permute-start | bytes 884744 | tf_op jit(solution)/shard_map/ppermute | solution.py:56
  36.1 5.6 %collective-permute-done = bf16[384,384]{1,0:T(8,128)(2,1)S(1)} collective-permute-done((bf16[384,384]{1,0:T(8,128)(2,1)S(1)}, bf16[384,384]{1,0:T(8,128)(2,1)S(1)}, u32[]{:S(2)}, u32[]{:S(2)}) %collective-permute-start) | collective-permute-done | bytes 294944 | tf_op jit(solution)/shard_map/ppermute | solution.py:53
  42.5 3.7 %collective-permute-start.3 = (bf16[384,384]{1,0:T(8,128)(2,1)S(1)}, bf16[384,384]{1,0:T(8,128)(2,1)}, u32[]{:S(2)}, u32[]{:S(2)}) collective-permute-start(bf16[384,384]{1,0:T(8,128)(2,1)S(1)} %collective-permute-done.1), channel_id=1, source_target_pairs={{0,135},{1,0},{2,1},{3,2},{4,3},{5,4},{6,5},{7,6},{128,7},{129,128... | collective-permute-start | bytes 884744 | tf_op jit(solution)/shard_map/ppermute | solution.py:56
  46.2 4.1 %collective-permute-done.2 = bf16[384,384]{1,0:T(8,128)(2,1)} collective-permute-done((bf16[384,384]{1,0:T(8,128)(2,1)S(1)}, bf16[384,384]{1,0:T(8,128)(2,1)}, u32[]{:S(2)}, u32[]{:S(2)}) %collective-permute-start.2) | collective-permute-done | bytes 294944 | tf_op jit(solution)/shard_map/ppermute | solution.py:53
  50.3 1.9 collective-permute-done.3
  52.2 3.8 %collective-permute-start.5 = (bf16[384,384]{1,0:T(8,128)(2,1)}, bf16[384,384]{1,0:T(8,128)(2,1)}, u32[]{:S(2)}, u32[]{:S(2)}) collective-permute-start(bf16[384,384]{1,0:T(8,128)(2,1)} %collective-permute-done.3), channel_id=1, source_target_pairs={{0,135},{1,0},{2,1},{3,2},{4,3},{5,4},{6,5},{7,6},{128,7},{129,128... | collective-permute-start | bytes 884744 | tf_op jit(solution)/shard_map/ppermute | solution.py:56
  56.0 3.1 %collective-permute-done.4 = bf16[384,384]{1,0:T(8,128)(2,1)} collective-permute-done((bf16[384,384]{1,0:T(8,128)(2,1)}, bf16[384,384]{1,0:T(8,128)(2,1)}, u32[]{:S(2)}, u32[]{:S(2)}) %collective-permute-start.4) | collective-permute-done | bytes 294944 | tf_op jit(solution)/shard_map/ppermute | solution.py:53
  59.8 2.7 %collective-permute-done.5 = bf16[384,384]{1,0:T(8,128)(2,1)} collective-permute-done((bf16[384,384]{1,0:T(8,128)(2,1)}, bf16[384,384]{1,0:T(8,128)(2,1)}, u32[]{:S(2)}, u32[]{:S(2)}) %collective-permute-start.5) | collective-permute-done | bytes 294944 | tf_op jit(solution)/shard_map/ppermute | solution.py:56
  62.6 3.7 %collective-permute-start.7 = (bf16[384,384]{1,0:T(8,128)(2,1)}, bf16[384,384]{1,0:T(8,128)(2,1)S(1)}, u32[]{:S(2)}, u32[]{:S(2)}) collective-permute-start(bf16[384,384]{1,0:T(8,128)(2,1)} %collective-permute-done.5), channel_id=1, source_target_pairs={{0,135},{1,0},{2,1},{3,2},{4,3},{5,4},{6,5},{7,6},{128,7},{129,128... | collective-permute-start | bytes 884744 | tf_op jit(solution)/shard_map/ppermute | solution.py:56
  66.3 1.5 collective-permute-done.6
  70.0 3.2 %collective-permute-done.7 = bf16[384,384]{1,0:T(8,128)(2,1)S(1)} collective-permute-done((bf16[384,384]{1,0:T(8,128)(2,1)}, bf16[384,384]{1,0:T(8,128)(2,1)S(1)}, u32[]{:S(2)}, u32[]{:S(2)}) %collective-permute-start.7) | collective-permute-done | bytes 294944 | tf_op jit(solution)/shard_map/ppermute | solution.py:56
  73.1 3.6 %collective-permute-start.9 = (bf16[384,384]{1,0:T(8,128)(2,1)S(1)}, bf16[384,384]{1,0:T(8,128)(2,1)S(1)}, u32[]{:S(2)}, u32[]{:S(2)}) collective-permute-start(bf16[384,384]{1,0:T(8,128)(2,1)S(1)} %collective-permute-done.7), channel_id=1, source_target_pairs={{0,135},{1,0},{2,1},{3,2},{4,3},{5,4},{6,5},{7,6},{128,7},{129,128... | collective-permute-start | bytes 884744 | tf_op jit(solution)/shard_map/ppermute | solution.py:56
  79.0 4.5 %collective-permute-done.9 = bf16[384,384]{1,0:T(8,128)(2,1)S(1)} collective-permute-done((bf16[384,384]{1,0:T(8,128)(2,1)S(1)}, bf16[384,384]{1,0:T(8,128)(2,1)S(1)}, u32[]{:S(2)}, u32[]{:S(2)}) %collective-permute-start.9) | collective-permute-done | bytes 294944 | tf_op jit(solution)/shard_map/ppermute | solution.py:56
  83.5 3.7 %collective-permute-start.11 = (bf16[384,384]{1,0:T(8,128)(2,1)S(1)}, bf16[384,384]{1,0:T(8,128)(2,1)S(1)}, u32[]{:S(2)}, u32[]{:S(2)}) collective-permute-start(bf16[384,384]{1,0:T(8,128)(2,1)S(1)} %collective-permute-done.9), channel_id=1, source_target_pairs={{0,135},{1,0},{2,1},{3,2},{4,3},{5,4},{6,5},{7,6},{128,7},{129,128... | collective-permute-start | bytes 884744 | tf_op jit(solution)/shard_map/ppermute | solution.py:56
  87.7 6.0 %collective-permute-done.11 = bf16[384,384]{1,0:T(8,128)(2,1)S(1)} collective-permute-done((bf16[384,384]{1,0:T(8,128)(2,1)S(1)}, bf16[384,384]{1,0:T(8,128)(2,1)S(1)}, u32[]{:S(2)}, u32[]{:S(2)}) %collective-permute-start.11) | collective-permute-done | bytes 294944 | tf_op jit(solution)/shard_map/ppermute | solution.py:56
  93.7 3.7 %collective-permute-start.13 = (bf16[384,384]{1,0:T(8,128)(2,1)S(1)}, bf16[384,384]{1,0:T(8,128)(2,1)S(1)}, u32[]{:S(2)}, u32[]{:S(2)}) collective-permute-start(bf16[384,384]{1,0:T(8,128)(2,1)S(1)} %collective-permute-done.11), channel_id=1, source_target_pairs={{0,135},{1,0},{2,1},{3,2},{4,3},{5,4},{6,5},{7,6},{128,7},{129,128... | collective-permute-start | bytes 884744 | tf_op jit(solution)/shard_map/ppermute | solution.py:56
  97.8 6.2 %collective-permute-done.13 = bf16[384,384]{1,0:T(8,128)(2,1)S(1)} collective-permute-done((bf16[384,384]{1,0:T(8,128)(2,1)S(1)}, bf16[384,384]{1,0:T(8,128)(2,1)S(1)}, u32[]{:S(2)}, u32[]{:S(2)}) %collective-permute-start.13) | collective-permute-done | bytes 294944 | tf_op jit(solution)/shard_map/ppermute | solution.py:56
  104.0 3.5 %collective-permute-done.14 = bf16[384,384]{1,0:T(8,128)(2,1)S(1)} collective-permute-done((bf16[384,384]{1,0:T(8,128)(2,1)S(1)}, bf16[384,384]{1,0:T(8,128)(2,1)S(1)}, u32[]{:S(2)}, u32[]{:S(2)}) %collective-permute-start.14) | collective-permute-done | bytes 294944 | tf_op jit(solution)/shard_map/ppermute | solution.py:53
  107.6 2.2 copy-done.1
  109.8 1.4 fusion.1
  111.2 10.5 %convolution_convert_fusion = bf16[384,6144]{1,0:T(8,128)(2,1)} fusion(bf16[1,256,6144]{2,1,0:T(8,128)(2,1)S(1)} %copy-done, f32[384,256]{1,0:T(8,128)S(1)} %fusion.1, bf16[384,6144]{1,0:T(8,128)(2,1)} %copy-done.1, bf16[1,6144,256]{2,1,0:T(8,128)(2,1)} %param.9), kind=kOutput, calls=%fused_computation.2 | convolution fusion | flops 2418868224 | bytes 16121856 | tf_op jit(solution)/shard_map/dot_general | solution.py:64
  121.8 6.7 %copy.52 = bf16[384,6144]{0,1:T(8,128)(2,1)} copy(bf16[384,6144]{1,0:T(8,128)(2,1)} %convolution_convert_fusion) | data formatting | bytes 9437184
  130.1 1.9 fusion.13
  132.0 2.0 gather_fusion.1
  134.4 64.6 %reduce-scatter.4.cloned.1.call-done = bf16[384,384]{1,0:T(8,128)(2,1)} async-done(((bf16[6144,384]{1,0:T(8,128)(2,1)}), bf16[384,384]{1,0:T(8,128)(2,1)}) %reduce-scatter.4.cloned.1.call-update) | async-done | bytes 294928
  198.9 1.8 copy.53
  200.8 6.6 %all-to-all-start.1 = ((bf16[16,24,384]{2,1,0:T(8,128)(2,1)}), bf16[16,24,384]{2,1,0:T(8,128)(2,1)S(1)}, u32[]{:S(2)}, u32[]{:S(2)}) async-start(bf16[16,24,384]{2,1,0:T(8,128)(2,1)} %bitcast.46), calls=%async_computation.1 | async-start | bytes 589824 | tf_op jit(solution)/shard_map/all_to_all | solution.py:70
  207.4 8.4 %all-to-all-done.1 = bf16[16,24,384]{2,1,0:T(8,128)(2,1)S(1)} async-done(((bf16[16,24,384]{2,1,0:T(8,128)(2,1)}), bf16[16,24,384]{2,1,0:T(8,128)(2,1)S(1)}, u32[]{:S(2)}, u32[]{:S(2)}) %all-to-all-start.1) | async-done | bytes 294944 | tf_op jit(solution)/shard_map/all_to_all | solution.py:70
  215.8 1.8 gather_fusion
  218.6 1.3 multiply_reduce_fusion
  (89 shorter events, 16.4 us)
Async XLA Ops:
  6.5 104.7 %copy-start = (bf16[1,256,6144]{2,1,0:T(8,128)(2,1)S(1)}, bf16[1,256,6144]{2,1,0:T(8,128)(2,1)}, u32[]{:S(2)}) copy-start(bf16[1,256,6144]{2,1,0:T(8,128)(2,1)} %param.11) | copy-start | bytes 9437188
  6.5 192.4 %reduce-scatter.4.cloned.1.call-start = ((), (), s32[]{:S(2)}) async-start(), calls=%async_computation.3 | async-start | bytes 5013504
  7.6 1.4 copy-start.10
  11.7 0.6 copy-start.8
  28.8 12.8 %collective-permute-start = (bf16[384,384]{1,0:T(8,128)(2,1)S(1)}, bf16[384,384]{1,0:T(8,128)(2,1)S(1)}, u32[]{:S(2)}, u32[]{:S(2)}) collective-permute-start(bf16[384,384]{1,0:T(8,128)(2,1)S(1)} %bitcast.47), channel_id=1, source_target_pairs={{0,1},{1,2},{2,3},{3,4},{4,5},{5,6},{6,7},{7,128},{128,129},{129,1... | collective-permute-start | bytes 884744 | tf_op jit(solution)/shard_map/ppermute | solution.py:53
  30.4 11.3 %collective-permute-start.1 = (bf16[384,384]{1,0:T(8,128)(2,1)S(1)}, bf16[384,384]{1,0:T(8,128)(2,1)S(1)}, u32[]{:S(2)}, u32[]{:S(2)}) collective-permute-start(bf16[384,384]{1,0:T(8,128)(2,1)S(1)} %bitcast.48), channel_id=1, source_target_pairs={{0,135},{1,0},{2,1},{3,2},{4,3},{5,4},{6,5},{7,6},{128,7},{129,128... | collective-permute-start | bytes 884744 | tf_op jit(solution)/shard_map/ppermute | solution.py:56
  41.6 10.5 %copy-start.4 = (bf16[384,384]{1,0:T(8,128)(2,1)}, bf16[384,384]{1,0:T(8,128)(2,1)S(1)}, u32[]{:S(2)}) copy-start(bf16[384,384]{1,0:T(8,128)(2,1)S(1)} %collective-permute-done) | copy-start | bytes 884740
  41.6 8.6 %collective-permute-start.2 = (bf16[384,384]{1,0:T(8,128)(2,1)S(1)}, bf16[384,384]{1,0:T(8,128)(2,1)}, u32[]{:S(2)}, u32[]{:S(2)}) collective-permute-start(bf16[384,384]{1,0:T(8,128)(2,1)S(1)} %collective-permute-done), channel_id=1, source_target_pairs={{0,1},{1,2},{2,3},{3,4},{4,5},{5,6},{6,7},{7,128},{128,129},{129,1... | collective-permute-start | bytes 884744 | tf_op jit(solution)/shard_map/ppermute | solution.py:53
  41.8 0.7 copy-start.2
  42.5 9.7 %collective-permute-start.3 = (bf16[384,384]{1,0:T(8,128)(2,1)S(1)}, bf16[384,384]{1,0:T(8,128)(2,1)}, u32[]{:S(2)}, u32[]{:S(2)}) collective-permute-start(bf16[384,384]{1,0:T(8,128)(2,1)S(1)} %collective-permute-done.1), channel_id=1, source_target_pairs={{0,135},{1,0},{2,1},{3,2},{4,3},{5,4},{6,5},{7,6},{128,7},{129,128... | collective-permute-start | bytes 884744 | tf_op jit(solution)/shard_map/ppermute | solution.py:56
  50.3 8.8 %collective-permute-start.4 = (bf16[384,384]{1,0:T(8,128)(2,1)}, bf16[384,384]{1,0:T(8,128)(2,1)}, u32[]{:S(2)}, u32[]{:S(2)}) collective-permute-start(bf16[384,384]{1,0:T(8,128)(2,1)} %collective-permute-done.2), channel_id=1, source_target_pairs={{0,1},{1,2},{2,3},{3,4},{4,5},{5,6},{6,7},{7,128},{128,129},{129,1... | collective-permute-start | bytes 884744 | tf_op jit(solution)/shard_map/ppermute | solution.py:53
  52.2 10.4 %collective-permute-start.5 = (bf16[384,384]{1,0:T(8,128)(2,1)}, bf16[384,384]{1,0:T(8,128)(2,1)}, u32[]{:S(2)}, u32[]{:S(2)}) collective-permute-start(bf16[384,384]{1,0:T(8,128)(2,1)} %collective-permute-done.3), channel_id=1, source_target_pairs={{0,135},{1,0},{2,1},{3,2},{4,3},{5,4},{6,5},{7,6},{128,7},{129,128... | collective-permute-start | bytes 884744 | tf_op jit(solution)/shard_map/ppermute | solution.py:56
  56.0 3.8 %copy-start.5 = (bf16[384,384]{1,0:T(8,128)(2,1)S(1)}, bf16[384,384]{1,0:T(8,128)(2,1)}, u32[]{:S(2)}) copy-start(bf16[384,384]{1,0:T(8,128)(2,1)} %copy-done.4) | copy-start | bytes 884740
  56.0 10.3 %copy-start.3 = (bf16[384,384]{1,0:T(8,128)(2,1)S(1)}, bf16[384,384]{1,0:T(8,128)(2,1)}, u32[]{:S(2)}) copy-start(bf16[384,384]{1,0:T(8,128)(2,1)} %copy-done.2) | copy-start | bytes 884740
  59.1 8.7 %collective-permute-start.6 = (bf16[384,384]{1,0:T(8,128)(2,1)}, bf16[384,384]{1,0:T(8,128)(2,1)S(1)}, u32[]{:S(2)}, u32[]{:S(2)}) collective-permute-start(bf16[384,384]{1,0:T(8,128)(2,1)} %collective-permute-done.4), channel_id=1, source_target_pairs={{0,1},{1,2},{2,3},{3,4},{4,5},{5,6},{6,7},{7,128},{128,129},{129,1... | collective-permute-start | bytes 884744 | tf_op jit(solution)/shard_map/ppermute | solution.py:53
  59.7 50.1 %copy-start.11 = (bf16[1,6144,256]{2,1,0:T(8,128)(2,1)S(1)}, bf16[1,6144,256]{2,1,0:T(8,128)(2,1)}, u32[]{:S(2)}) copy-start(bf16[1,6144,256]{2,1,0:T(8,128)(2,1)} %param.10) | copy-start | bytes 9437188
  62.6 10.6 %collective-permute-start.7 = (bf16[384,384]{1,0:T(8,128)(2,1)}, bf16[384,384]{1,0:T(8,128)(2,1)S(1)}, u32[]{:S(2)}, u32[]{:S(2)}) collective-permute-start(bf16[384,384]{1,0:T(8,128)(2,1)} %collective-permute-done.5), channel_id=1, source_target_pairs={{0,135},{1,0},{2,1},{3,2},{4,3},{5,4},{6,5},{7,6},{128,7},{129,128... | collective-permute-start | bytes 884744 | tf_op jit(solution)/shard_map/ppermute | solution.py:56
  67.8 9.9 %collective-permute-start.8 = (bf16[384,384]{1,0:T(8,128)(2,1)S(1)}, bf16[384,384]{1,0:T(8,128)(2,1)S(1)}, u32[]{:S(2)}, u32[]{:S(2)}) collective-permute-start(bf16[384,384]{1,0:T(8,128)(2,1)S(1)} %collective-permute-done.6), channel_id=1, source_target_pairs={{0,1},{1,2},{2,3},{3,4},{4,5},{5,6},{6,7},{7,128},{128,129},{129,1... | collective-permute-start | bytes 884744 | tf_op jit(solution)/shard_map/ppermute | solution.py:53
  73.1 10.4 %collective-permute-start.9 = (bf16[384,384]{1,0:T(8,128)(2,1)S(1)}, bf16[384,384]{1,0:T(8,128)(2,1)S(1)}, u32[]{:S(2)}, u32[]{:S(2)}) collective-permute-start(bf16[384,384]{1,0:T(8,128)(2,1)S(1)} %collective-permute-done.7), channel_id=1, source_target_pairs={{0,135},{1,0},{2,1},{3,2},{4,3},{5,4},{6,5},{7,6},{128,7},{129,128... | collective-permute-start | bytes 884744 | tf_op jit(solution)/shard_map/ppermute | solution.py:56
  77.8 9.8 %collective-permute-start.10 = (bf16[384,384]{1,0:T(8,128)(2,1)S(1)}, bf16[384,384]{1,0:T(8,128)(2,1)S(1)}, u32[]{:S(2)}, u32[]{:S(2)}) collective-permute-start(bf16[384,384]{1,0:T(8,128)(2,1)S(1)} %collective-permute-done.8), channel_id=1, source_target_pairs={{0,1},{1,2},{2,3},{3,4},{4,5},{5,6},{6,7},{7,128},{128,129},{129,1... | collective-permute-start | bytes 884744 | tf_op jit(solution)/shard_map/ppermute | solution.py:53
  83.5 10.2 %collective-permute-start.11 = (bf16[384,384]{1,0:T(8,128)(2,1)S(1)}, bf16[384,384]{1,0:T(8,128)(2,1)S(1)}, u32[]{:S(2)}, u32[]{:S(2)}) collective-permute-start(bf16[384,384]{1,0:T(8,128)(2,1)S(1)} %collective-permute-done.9), channel_id=1, source_target_pairs={{0,135},{1,0},{2,1},{3,2},{4,3},{5,4},{6,5},{7,6},{128,7},{129,128... | collective-permute-start | bytes 884744 | tf_op jit(solution)/shard_map/ppermute | solution.py:56
  87.5 10.0 %collective-permute-start.12 = (bf16[384,384]{1,0:T(8,128)(2,1)S(1)}, bf16[384,384]{1,0:T(8,128)(2,1)S(1)}, u32[]{:S(2)}, u32[]{:S(2)}) collective-permute-start(bf16[384,384]{1,0:T(8,128)(2,1)S(1)} %collective-permute-done.10), channel_id=1, source_target_pairs={{0,1},{1,2},{2,3},{3,4},{4,5},{5,6},{6,7},{7,128},{128,129},{129,1... | collective-permute-start | bytes 884744 | tf_op jit(solution)/shard_map/ppermute | solution.py:53
  93.7 10.2 %collective-permute-start.13 = (bf16[384,384]{1,0:T(8,128)(2,1)S(1)}, bf16[384,384]{1,0:T(8,128)(2,1)S(1)}, u32[]{:S(2)}, u32[]{:S(2)}) collective-permute-start(bf16[384,384]{1,0:T(8,128)(2,1)S(1)} %collective-permute-done.11), channel_id=1, source_target_pairs={{0,135},{1,0},{2,1},{3,2},{4,3},{5,4},{6,5},{7,6},{128,7},{129,128... | collective-permute-start | bytes 884744 | tf_op jit(solution)/shard_map/ppermute | solution.py:56
  97.5 10.0 %collective-permute-start.14 = (bf16[384,384]{1,0:T(8,128)(2,1)S(1)}, bf16[384,384]{1,0:T(8,128)(2,1)S(1)}, u32[]{:S(2)}, u32[]{:S(2)}) collective-permute-start(bf16[384,384]{1,0:T(8,128)(2,1)S(1)} %collective-permute-done.12), channel_id=1, source_target_pairs={{0,1},{1,2},{2,3},{3,4},{4,5},{5,6},{6,7},{7,128},{128,129},{129,1... | collective-permute-start | bytes 884744 | tf_op jit(solution)/shard_map/ppermute | solution.py:53
  107.6 2.2 copy-start.1
  128.5 0.7 copy-start.9
  128.5 0.8 copy-start.7
  128.5 1.6 copy-start.6
  200.8 15.0 %all-to-all-start.1 = ((bf16[16,24,384]{2,1,0:T(8,128)(2,1)}), bf16[16,24,384]{2,1,0:T(8,128)(2,1)S(1)}, u32[]{:S(2)}, u32[]{:S(2)}) async-start(bf16[16,24,384]{2,1,0:T(8,128)(2,1)} %bitcast.46), calls=%async_computation.1 | async-start | bytes 589824 | tf_op jit(solution)/shard_map/all_to_all | solution.py:70
Sparse Core Ops, SparseCore 0:
  128.6 70.2 reduce-scatter.3
